TPU v7x, 32 devices: a whole 2x2x4 slice. The times are simulated.
32 devices in a mesh: shot: 4 (over y, x), rcv: 8 (over z, core).
Axes of the slice: x: 2, y: 2, z: 4, core: 2. Of those that a mesh axis runs over, the one named last changes fastest.
Arguments:
- modeled: bfloat16 [2, 32, 4, 64, 512], P(None, 'shot', None, 'rcv'), may hold values from -9 to 9
- observed: bfloat16 [2, 4, 32, 64, 512], P(None, 'shot', 'rcv'), may hold values from -60 to 60
- mask: int32 [32, 4, 64], P('shot', None, 'rcv'), may hold values 0 or 1
- shot_order: int32 [32], replicated, may hold values from 0 to 31, as said below
- line_of_slot: int32 [4], replicated, may hold values from 0 to 3, as said below
- coupling: bfloat16 [2, 512, 512], replicated, may hold values from -0.25 to 0.25
- wavelet: float32 [2, 512], replicated, may hold values from -4 to 4
- damping: float32 [512], replicated, may hold values from 2048 to 32768
Outputs:
- new_wavelet: float32 [2, 512], replicated
- residual_out: bfloat16 [2, 32, 4, 64, 512], P(None, 'shot', None, 'rcv')
Inputs may be any that keep to these rules, and one draw needn't show every extreme that they name: Group g holds the shots shot_order[g * 8] to shot_order[(g + 1) * 8 - 1]; each shot number appears once. `line_of_slot`: each line appears in exactly one slot.
All inputs are finite; a program needn't handle non-finite values. No bound on the sum of `mask` on one device may be relied on, other than what follows from the above.
Results may differ from a plain program's by a relative error of at most 0.00045.
Values may be sent and summed in bfloat16 or wider, within the bound.
A program may use at most 64 MiB of HBM per device.

v0:
```python
import jax
import jax.numpy as jnp
from jax import lax
from jax.sharding import PartitionSpec as P


def weigh(trace, coupling):
    real_part = jnp.dot(trace[0], coupling[0], preferred_element_type=jnp.float32) - jnp.dot(
        trace[1], coupling[1], preferred_element_type=jnp.float32
    )
    imag_part = jnp.dot(trace[0], coupling[1], preferred_element_type=jnp.float32) + jnp.dot(
        trace[1], coupling[0], preferred_element_type=jnp.float32
    )
    return jnp.stack([real_part, imag_part])


def per_device(modeled, observed, mask, shot_order, line_of_slot, coupling, wavelet, damping):
    group_size = modeled.shape[1]
    line_count = modeled.shape[2]
    slot_count = lax.axis_size("shot")
    stored = observed[:, 0]
    spread = lax.all_to_all(stored, "rcv", split_axis=2, concat_axis=1, tiled=True)
    grouped = jnp.take(spread, shot_order, axis=1)
    grouped = grouped.reshape(2, slot_count, group_size, grouped.shape[2], grouped.shape[3])
    arrived = lax.all_to_all(grouped, "shot", split_axis=1, concat_axis=1, tiled=True)
    inverse = (
        jnp.zeros((line_count,), jnp.int32)
        .at[line_of_slot]
        .set(jnp.arange(line_count, dtype=jnp.int32))
    )
    by_line = jnp.transpose(jnp.take(arrived, inverse, axis=1), (0, 2, 1, 3, 4))
    wd = weigh(by_line, coupling)
    wg = weigh(modeled, coupling)
    live = mask.astype(jnp.float32)[..., None]
    res_re = live * (wd[0] - (wavelet[0] * wg[0] - wavelet[1] * wg[1]))
    res_im = live * (wd[1] - (wavelet[0] * wg[1] + wavelet[1] * wg[0]))
    num_re = jnp.sum(wg[0] * res_re + wg[1] * res_im, axis=(0, 1, 2))
    num_im = jnp.sum(wg[0] * res_im - wg[1] * res_re, axis=(0, 1, 2))
    den = jnp.sum(live * (wg[0] * wg[0] + wg[1] * wg[1]), axis=(0, 1, 2))
    numerator = jnp.stack([num_re, num_im])
    numerator, den = lax.psum((numerator, den), ("shot", "rcv"))
    new_wavelet = wavelet + numerator / (den + damping)[None, :]
    out_re = live * (wd[0] - (new_wavelet[0] * wg[0] - new_wavelet[1] * wg[1]))
    out_im = live * (wd[1] - (new_wavelet[0] * wg[1] + new_wavelet[1] * wg[0]))
    return (new_wavelet, jnp.stack([out_re, out_im]).astype(jnp.bfloat16))


def solution(mesh):
    placed = (
        P(None, "shot", None, "rcv", None),
        P(None, "shot", "rcv", None, None),
        P("shot", None, "rcv"),
        P(),
        P(),
        P(),
        P(),
        P(),
    )
    return jax.shard_map(
        per_device,
        mesh=mesh,
        in_specs=placed,
        out_specs=(P(), P(None, "shot", None, "rcv", None)),
        check_vma=False,
    )
```

profile of v0, /device:TPU:0, one launch (start us, length us, event | category | flops | bytes accessed | tf_op | source)
XLA Modules:
  0.0 82.2 jit_solution(1885239426793906169)
XLA Ops:
  0.6 0.0 copy-start
  0.6 2.3 %copy.30 = bf16[2,1,4,64,512]{4,2,0,3,1:T(4,128)(2,1)} copy(bf16[2,1,4,64,512]{4,3,2,1,0:T(8,128)(2,1)} %param.9) | data formatting | bytes 1048576 | tf_op args[1]
  3.0 6.5 %all-to-all-start = ((bf16[2,4,64,512]{3,1,0,2:T(4,128)(2,1)}), bf16[2,4,64,512]{3,1,0,2:T(4,128)(2,1)S(1)}, u32[]{:S(2)}, u32[]{:S(2)}) async-start(bf16[2,4,64,512]{3,1,0,2:T(4,128)(2,1)} %bitcast.71), calls=%async_computation | async-start | bytes 1048576 | tf_op jit(solution)/shard_map/all_to_all | solution.py:22
  9.5 0.0 copy-done.7
  9.5 0.0 copy-start.8
  9.5 0.6 copy-done.8
  10.1 0.1 broadcast_in_dim.31
  10.2 0.6 scatter_custom_fusion
  10.9 0.1 copy-done.3
  10.9 0.0 copy-done
  10.9 1.1 %fusion.2 = f32[8,4,8,512]{3,2,1,0:T(8,128)} fusion(bf16[2,512,512]{2,1,0:T(8,128)(2,1)S(1)} %copy-done, bf16[2,8,4,8,512]{4,3,2,1,0:T(8,128)(2,1)S(1)} %copy-done.1), kind=kOutput, calls=%fused_computation.10 | convolution fusion | flops 134217728 | bytes 1310720 | tf_op jit(solution)/shard_map/dot_general | solution.py:11
  12.0 0.3 fusion.10
  12.3 12.5 %all-to-all-done = bf16[2,4,64,512]{3,1,0,2:T(4,128)(2,1)S(1)} async-done(((bf16[2,4,64,512]{3,1,0,2:T(4,128)(2,1)}), bf16[2,4,64,512]{3,1,0,2:T(4,128)(2,1)S(1)}, u32[]{:S(2)}, u32[]{:S(2)}) %all-to-all-start) | async-done | bytes 524320 | tf_op jit(solution)/shard_map/all_to_all | solution.py:22
  24.8 0.2 copy.29
  25.0 0.6 gather_fusion
  25.6 0.9 %copy_select_fusion.1 = bf16[2,4,8,8,512]{4,3,2,0,1:T(8,128)(2,1)} fusion(bf16[2,4,8,8,512]{4,3,0,2,1:T(8,128)(2,1)S(1)} %bitcast.75, pred[4,8]{1,0:T(4,128)(4,1)S(1)} %broadcast_in_dim.31), kind=kLoop, calls=%fused_computation.22 | loop fusion | flops 262144 | bytes 1048608 | tf_op jit(solution)/shard_map/jit(_take)/select_n | solution.py:23
  26.5 3.8 %all-to-all-start.1 = ((bf16[2,4,8,8,512]{4,3,2,0,1:T(8,128)(2,1)}), bf16[2,4,8,8,512]{4,3,2,0,1:T(8,128)(2,1)S(1)}, u32[]{:S(2)}, u32[]{:S(2)}) async-start(bf16[2,4,8,8,512]{4,3,2,0,1:T(8,128)(2,1)} %copy_select_fusion.1), calls=%async_computation.1 | async-start | bytes 1048576 | tf_op jit(solution)/shard_map/all_to_all | solution.py:25
  30.4 0.3 convolution_subtract_fusion.1
  30.7 7.4 %all-to-all-done.1 = bf16[2,4,8,8,512]{4,3,2,0,1:T(8,128)(2,1)S(1)} async-done(((bf16[2,4,8,8,512]{4,3,2,0,1:T(8,128)(2,1)}), bf16[2,4,8,8,512]{4,3,2,0,1:T(8,128)(2,1)S(1)}, u32[]{:S(2)}, u32[]{:S(2)}) %all-to-all-start.1) | async-done | bytes 524320 | tf_op jit(solution)/shard_map/all_to_all | solution.py:25
  38.1 0.6 gather_fusion.1
  38.7 0.1 fusion.12
  38.8 0.3 fusion
  39.1 0.3 fusion.8
  39.4 0.3 convolution_add_fusion
  39.8 0.3 convolution_subtract_fusion
  40.1 0.7 copy-done.2
  40.8 1.4 %add_reduce_fusion = (f32[512]{0:T(512)S(1)}, f32[512]{0:T(512)S(1)}, f32[512]{0:T(512)S(1)}, f32[8,4,8,512]{3,2,1,0:T(8,128)}) fusion(f32[8,4,8,512]{3,2,1,0:T(8,128)S(1)} %convolution_add_fusion, f32[8,4,8,512]{3,2,1,0:T(8,128)S(1)} %convolution_subtract_fusion.1, f32[8,4,8,512]{3,2,1,0:T(8,128)S(1)} %convolution_subtract_fusion, f32[512]{0:T(512)S(1)} %bitcast.79, ...), kind=kOutput, calls=%fused_computation.29 | convolution fusion | flops 137361920 | bytes 3434496 | tf_op jit(solution)/shard_map/dot_general | solution.py:11
  42.2 37.2 %all-reduce = (f32[2,512]{1,0:T(2,128)S(1)}, f32[512]{0:T(512)S(1)}) all-reduce(f32[2,512]{1,0:T(2,128)S(1)} %pad_maximum_fusion.1, f32[512]{0:T(512)S(1)} %get-tuple-element.4), channel_id=1, replica_groups=mesh['shot'=4,'rcv'=8] {'shot','rcv'}, use_global_device_ids=true, to_apply=%region_3.4 | all-reduce | flops 1536 | bytes 12288 | tf_op jit(solution)/shard_map/psum | solution.py:41
  79.5 0.0 copy-start.4
  79.5 0.6 copy-done.4
  80.1 1.3 %fusion.21 = (bf16[1,8,4,8,512]{4,3,2,1,0:T(8,128)(2,1)S(1)}, bf16[1,8,4,8,512]{4,3,2,1,0:T(8,128)(2,1)S(1)}) fusion(f32[8,4,8,512]{3,2,1,0:T(8,128)S(1)} %convolution_subtract_fusion, f32[8,4,8,512]{3,2,1,0:T(8,128)} %get-tuple-element.13, f32[8,4,8,512]{3,2,1,0:T(8,128)S(1)} %convolution_subtract_fusion.1, f32[512]{0:T(512)S(1)} %bitcast.77, ...), kind=kLoop, calls=%fused_computation.40 | loop fusion | flops 1572864 | bytes 2626560 | tf_op jit(solution)/shard_map/stack | solution.py:45
  81.4 0.8 %pad_maximum_fusion = bf16[2,8,4,8,512]{4,3,2,1,0:T(8,128)(2,1)} fusion(bf16[1,8,4,8,512]{4,3,2,1,0:T(8,128)(2,1)S(1)} %get-tuple-element.8, bf16[1,8,4,8,512]{4,3,2,1,0:T(8,128)(2,1)S(1)} %get-tuple-element.7), kind=kLoop, calls=%fused_computation.7 | loop fusion | flops 262144 | bytes 1048576 | tf_op jit(solution)/shard_map/stack | solution.py:45
  (25 shorter events, 0.2 us)
Async XLA Ops:
  0.6 10.3 %copy-start = (bf16[2,512,512]{2,1,0:T(8,128)(2,1)S(1)}, bf16[2,512,512]{2,1,0:T(8,128)(2,1)}, u32[]{:S(2)}) copy-start(bf16[2,512,512]{2,1,0:T(8,128)(2,1)} %param.13) | copy-start | bytes 3145732
  3.0 6.5 %copy-start.7 = (s32[32]{0:T(128)S(1)}, s32[32]{0:T(128)}, u32[]{:S(2)}) copy-start(s32[32]{0:T(128)} %param.11) | copy-start | bytes 388
  3.0 8.0 %copy-start.1 = (bf16[2,8,4,8,512]{4,3,2,1,0:T(8,128)(2,1)S(1)}, bf16[2,8,4,8,512]{4,3,2,1,0:T(8,128)(2,1)}, u32[]{:S(2)}) copy-start(bf16[2,8,4,8,512]{4,3,2,1,0:T(8,128)(2,1)} %param.8) | copy-start | bytes 1572868
  3.0 21.8 %all-to-all-start = ((bf16[2,4,64,512]{3,1,0,2:T(4,128)(2,1)}), bf16[2,4,64,512]{3,1,0,2:T(4,128)(2,1)S(1)}, u32[]{:S(2)}, u32[]{:S(2)}) async-start(bf16[2,4,64,512]{3,1,0,2:T(4,128)(2,1)} %bitcast.71), calls=%async_computation | async-start | bytes 1048576 | tf_op jit(solution)/shard_map/all_to_all | solution.py:22
  9.5 0.7 copy-start.8
  10.2 0.7 copy-start.3
  26.5 3.9 %copy-start.5 = (s32[8,4,8]{2,1,0:T(4,128)S(1)}, s32[8,4,8]{2,1,0:T(4,128)}, u32[]{:S(2)}) copy-start(s32[8,4,8]{2,1,0:T(4,128)} %param.10) | copy-start | bytes 3076
  26.5 11.6 %all-to-all-start.1 = ((bf16[2,4,8,8,512]{4,3,2,0,1:T(8,128)(2,1)}), bf16[2,4,8,8,512]{4,3,2,0,1:T(8,128)(2,1)S(1)}, u32[]{:S(2)}, u32[]{:S(2)}) async-start(bf16[2,4,8,8,512]{4,3,2,0,1:T(8,128)(2,1)} %copy_select_fusion.1), calls=%async_computation.1 | async-start | bytes 1048576 | tf_op jit(solution)/shard_map/all_to_all | solution.py:25
  39.7 1.0 %copy-start.2 = (f32[8,4,8,512]{3,2,1,0:T(8,128)S(1)}, f32[8,4,8,512]{3,2,1,0:T(8,128)}, u32[]{:S(2)}) copy-start(f32[8,4,8,512]{3,2,1,0:T(8,128)} %fusion.2) | copy-start | bytes 1572868
  40.8 38.7 %copy-start.6 = (f32[512]{0:T(512)S(1)}, f32[512]{0:T(512)}, u32[]{:S(2)}) copy-start(f32[512]{0:T(512)} %param.15) | copy-start | bytes 6148
  79.5 0.6 copy-start.4
where the time goes:
time: 83 us; the launch traced here: 82.2 us
  blocking collectives  37.2 us (45%)
  waiting for transfers between devices  19.8 us (24%)
  starting transfers between devices  10.3 us (12%)
  local copies, waits for them, and re-layouts  6.43 us (8%)
  matrix products  4.33 us (5%)
  other arithmetic  3.19 us (4%)
    psum x1, blocking collectives, per_device(): numerator, den = lax.psum((numerator, den), ('shot', 'rcv'))  37.2 us
    all_to_all x1, waiting for transfers between devices, per_device(): lax.all_to_all(stored, 'rcv', split_axis=2, concat_axis=1, tiled=True)  12.5 us
    all_to_all x1, waiting for transfers between devices, per_device(): lax.all_to_all(grouped, 'shot', split_axis=1, concat_axis=1, tiled=True)  7.38 us
    all_to_all x1, starting transfers between devices, per_device(): lax.all_to_all(stored, 'rcv', split_axis=2, concat_axis=1, tiled=True)  6.49 us
    unnamed x19, local copies, waits for them, and re-layouts  4.35 us
    all_to_all x1, starting transfers between devices, per_device(): lax.all_to_all(grouped, 'shot', split_axis=1, concat_axis=1, tiled=True)  3.85 us
    another operation x2, other arithmetic, per_device(): return (new_wavelet, jnp.stack([out_re, out_im]).astype(jnp.bfloat16))  2.1 us
    dot_general x2, matrix products, weigh(): jnp.dot(trace[1], coupling[0], preferred_element_type=jnp.float32)  1.73 us
  transfers between devices with their start and end apart: 2, of which 2 were waited for; matrix products, arithmetic and copies ran while one was open for 3% of the time, Pallas kernels for 0%

commit v1 on v0

v1 whole, which is shorter than its diff:
```python
import functools

import jax
import jax.numpy as jnp
from jax import lax
from jax.experimental import pallas as pl
from jax.experimental.pallas import tpu as pltpu
from jax.sharding import PartitionSpec as P

MESH = pl.DeviceIdType.MESH
PIECES = 2


def kernel(
    n_shot,
    n_rcv,
    modeled_hbm,
    observed_hbm,
    coupling_hbm,
    mask_ref,
    order_ref,
    slot_ref,
    wavelet_ref,
    damping_ref,
    new_ref,
    out_ref,
    mod,
    coup,
    spread,
    grouped,
    arrived,
    wg,
    wd,
    live,
    num_mine,
    num_rcv,
    num_group,
    num_shot,
    den_mine,
    den_rcv,
    den_group,
    den_shot,
    load_sem,
    own_sem,
    send1,
    recv1,
    send2,
    recv2,
    num_send1,
    num_recv1,
    num_send2,
    num_recv2,
    den_send1,
    den_recv1,
    den_send2,
    den_recv2,
):
    me_s = lax.axis_index("shot")
    me_r = lax.axis_index("rcv")
    size, lines, rows, freqs = modeled_hbm.shape[1:]
    held = observed_hbm.shape[2]
    parts = len(spread)
    width = spread[0].shape[2]

    rcv_peers = [lax.rem(me_r + d, n_rcv) for d in range(1, n_rcv)]
    shot_peers = [lax.rem(me_s + d, n_shot) for d in range(1, n_shot)]

    barrier = pltpu.get_barrier_semaphore()
    for r in rcv_peers:
        pl.semaphore_signal(barrier, inc=1, device_id=(me_s, r), device_id_type=MESH)
    for s in shot_peers:
        pl.semaphore_signal(barrier, inc=1, device_id=(s, me_r), device_id_type=MESH)

    load_mod = pltpu.make_async_copy(modeled_hbm, mod, load_sem.at[0])
    load_coup = pltpu.make_async_copy(coupling_hbm, coup, load_sem.at[1])
    load_mod.start()
    load_coup.start()

    def piece(t, r):
        c, h = divmod(t, parts // 2)
        return observed_hbm.at[
            c, 0, :, pl.ds(pl.multiple_of(r * rows, rows), rows), pl.ds(h * width, width)
        ]

    own = []
    for t in range(parts):
        copy = pltpu.make_async_copy(
            piece(t, me_r), spread[t].at[pl.ds(me_r * held, held)], own_sem.at[t]
        )
        copy.start()
        own.append(copy)

    pl.semaphore_wait(barrier, n_rcv + n_shot - 2)

    def spread_copy(t, d):
        return pltpu.make_async_remote_copy(
            src_ref=piece(t, rcv_peers[d - 1]),
            dst_ref=spread[t].at[pl.ds(me_r * held, held)],
            send_sem=send1.at[t, d - 1],
            recv_sem=recv1.at[t, d - 1],
            device_id=(me_s, rcv_peers[d - 1]),
            device_id_type=MESH,
        )

    def group_copy(t, d):
        return pltpu.make_async_remote_copy(
            src_ref=grouped.at[t, d - 1],
            dst_ref=arrived.at[t, me_s],
            send_sem=send2.at[t, d - 1],
            recv_sem=recv2.at[t, d - 1],
            device_id=(shot_peers[d - 1], me_r),
            device_id_type=MESH,
        )

    def rcv_sum(mine, slots, send, recv, start):
        for d in range(1, n_rcv):
            copy = pltpu.make_async_remote_copy(
                src_ref=mine,
                dst_ref=slots.at[me_r],
                send_sem=send.at[d - 1],
                recv_sem=recv.at[d - 1],
                device_id=(me_s, rcv_peers[d - 1]),
                device_id_type=MESH,
            )
            if start:
                copy.start()
            else:
                copy.wait()

    def shot_sum(mine, slots, send, recv, start):
        for d in range(1, n_shot):
            copy = pltpu.make_async_remote_copy(
                src_ref=mine,
                dst_ref=slots.at[me_s],
                send_sem=send.at[d - 1],
                recv_sem=recv.at[d - 1],
                device_id=(shot_peers[d - 1], me_r),
                device_id_type=MESH,
            )
            if start:
                copy.start()
            else:
                copy.wait()

    def total(slots, count):
        out = slots[0]
        for i in range(1, count):
            out = out + slots[i]
        return out

    for t in range(parts):
        for d in range(1, n_rcv):
            spread_copy(t, d).start()

    eye = (
        lax.broadcasted_iota(jnp.int32, (rows, rows), 0)
        == lax.broadcasted_iota(jnp.int32, (rows, rows), 1)
    )
    for p in range(size):
        for l in range(lines):
            flags = jnp.broadcast_to(mask_ref[p, l : l + 1, :].astype(jnp.float32), (rows, rows))
            column = jnp.sum(jnp.where(eye, flags, 0.0), axis=1, keepdims=True)
            live[p * lines + l] = jnp.broadcast_to(column, (rows, live.shape[2]))

    load_mod.wait()
    load_coup.wait()

    def dot(x, c):
        return jnp.dot(x, c, preferred_element_type=jnp.float32)

    tall = size * lines * rows
    x_re = mod[0].reshape(tall, freqs)
    x_im = mod[1].reshape(tall, freqs)
    wg[0] = (dot(x_re, coup[0]) - dot(x_im, coup[1])).reshape(size * lines, rows, freqs)
    wg[1] = (dot(x_re, coup[1]) + dot(x_im, coup[0])).reshape(size * lines, rows, freqs)

    wide = freqs // live.shape[2]

    def live_of(i):
        flag = live[i]
        return jnp.concatenate([flag] * wide, axis=1)

    den = jnp.zeros((rows, freqs), jnp.float32)
    for i in range(size * lines):
        den = den + live_of(i) * (wg[0, i] * wg[0, i] + wg[1, i] * wg[1, i])
    den_mine[...] = jnp.sum(den, axis=0, keepdims=True)
    den_rcv[me_r] = den_mine[...]
    rcv_sum(den_mine, den_rcv, den_send1, den_recv1, True)

    def multiply(t):
        c, h = divmod(t, parts // 2)
        for d in range(1, n_shot):
            group_copy(t, d).wait_recv()
        x = arrived[t].reshape(n_shot * size * rows, width)
        span = slice(h * width, (h + 1) * width)
        if c == 0:
            re = dot(x, coup[0, span, :]).reshape(n_shot, size * rows, freqs)
            im = dot(x, coup[1, span, :]).reshape(n_shot, size * rows, freqs)
        else:
            re = -dot(x, coup[1, span, :]).reshape(n_shot, size * rows, freqs)
            im = dot(x, coup[0, span, :]).reshape(n_shot, size * rows, freqs)
        if t == 0:
            wd[0] = re
            wd[1] = im
        else:
            wd[0] = wd[0] + re
            wd[1] = wd[1] + im

    for t in range(parts):
        own[t].wait()
        for d in range(1, n_rcv):
            spread_copy(t, d).wait_recv()
        for d in list(range(1, n_shot)) + [0]:
            group = shot_peers[d - 1] if d else me_s
            for p in range(0, size, 2):
                first = order_ref[group * size + p]
                second = order_ref[group * size + p + 1]
                pair = jnp.concatenate([spread[t][first], spread[t][second]], axis=0)
                if d:
                    grouped[t, d - 1, p * rows : (p + 2) * rows, :] = pair
                else:
                    arrived[t, me_s, p * rows : (p + 2) * rows, :] = pair
        for d in range(1, n_shot):
            group_copy(t, d).start()
        if t == parts - 1:
            rcv_sum(den_mine, den_rcv, den_send1, den_recv1, False)
            den_group[...] = total(den_rcv, n_rcv)
            den_shot[me_s] = den_group[...]
            shot_sum(den_group, den_shot, den_send2, den_recv2, True)
        if t > 0:
            multiply(t - 1)
    multiply(parts - 1)

    slot_of = []
    for l in range(lines):
        k = jnp.int32(0)
        for j in range(lines):
            k = jnp.where(slot_ref[j] == l, j, k)
        slot_of.append(k)

    w_re, w_im = wavelet_ref[0:1, :], wavelet_ref[1:2, :]
    num_re = jnp.zeros((rows, freqs), jnp.float32)
    num_im = jnp.zeros((rows, freqs), jnp.float32)
    for l in range(lines):
        for p in range(size):
            i = p * lines + l
            g_re, g_im, flag = wg[0, i], wg[1, i], live_of(i)
            at = slice(p * rows, (p + 1) * rows)
            res_re = flag * (wd[0, slot_of[l], at, :] - (w_re * g_re - w_im * g_im))
            res_im = flag * (wd[1, slot_of[l], at, :] - (w_re * g_im + w_im * g_re))
            num_re = num_re + (g_re * res_re + g_im * res_im)
            num_im = num_im + (g_re * res_im - g_im * res_re)
    num_mine[0:1, :] = jnp.sum(num_re, axis=0, keepdims=True)
    num_mine[1:2, :] = jnp.sum(num_im, axis=0, keepdims=True)
    num_rcv[me_r] = num_mine[...]
    rcv_sum(num_mine, num_rcv, num_send1, num_recv1, True)
    rcv_sum(num_mine, num_rcv, num_send1, num_recv1, False)
    num_group[...] = total(num_rcv, n_rcv)
    num_shot[me_s] = num_group[...]
    shot_sum(num_group, num_shot, num_send2, num_recv2, True)
    shot_sum(den_group, den_shot, den_send2, den_recv2, False)
    shot_sum(num_group, num_shot, num_send2, num_recv2, False)
    scale = total(den_shot, n_shot) + damping_ref[...]
    new = wavelet_ref[...] + total(num_shot, n_shot) / scale
    new_ref[...] = new

    n_re, n_im = new[0:1, :], new[1:2, :]
    for p in range(size):
        for l in range(lines):
            i = p * lines + l
            g_re, g_im, flag = wg[0, i], wg[1, i], live_of(i)
            at = slice(p * rows, (p + 1) * rows)
            out_re = flag * (wd[0, slot_of[l], at, :] - (n_re * g_re - n_im * g_im))
            out_im = flag * (wd[1, slot_of[l], at, :] - (n_re * g_im + n_im * g_re))
            out_ref[0, p, l] = out_re.astype(jnp.bfloat16)
            out_ref[1, p, l] = out_im.astype(jnp.bfloat16)

    for t in range(parts):
        for d in range(1, n_rcv):
            spread_copy(t, d).wait_send()
        for d in range(1, n_shot):
            group_copy(t, d).wait_send()


def solution(mesh):
    n_shot, n_rcv = mesh.shape["shot"], mesh.shape["rcv"]

    def per_device(modeled, observed, mask, shot_order, line_of_slot, coupling, wavelet, damping):
        _, size, lines, rows, freqs = modeled.shape
        shots = shot_order.shape[0]
        parts = 2 * PIECES
        width = freqs // PIECES
        f32, bf16 = jnp.float32, jnp.bfloat16
        dma = pltpu.SemaphoreType.DMA
        any_ = pl.BlockSpec(memory_space=pl.ANY)
        vmem = pl.BlockSpec(memory_space=pltpu.VMEM)
        smem = pl.BlockSpec(memory_space=pltpu.SMEM)
        return pl.pallas_call(
            functools.partial(kernel, n_shot, n_rcv),
            out_shape=(
                jax.ShapeDtypeStruct(wavelet.shape, f32),
                jax.ShapeDtypeStruct(modeled.shape, bf16),
            ),
            in_specs=[any_, any_, any_, vmem, smem, smem, vmem, vmem],
            out_specs=(vmem, vmem),
            scratch_shapes=[
                pltpu.VMEM(modeled.shape, bf16),
                pltpu.VMEM(coupling.shape, bf16),
                [pltpu.VMEM((shots, rows, width), bf16)] * parts,
                pltpu.VMEM((parts, n_shot - 1, size * rows, width), bf16),
                pltpu.VMEM((parts, n_shot, size * rows, width), bf16),
                pltpu.VMEM((2, size * lines, rows, freqs), f32),
                pltpu.VMEM((2, n_shot, size * rows, freqs), f32),
                pltpu.VMEM((size * lines, rows, 128), f32),
                pltpu.VMEM((2, freqs), f32),
                pltpu.VMEM((n_rcv, 2, freqs), f32),
                pltpu.VMEM((2, freqs), f32),
                pltpu.VMEM((n_shot, 2, freqs), f32),
                pltpu.VMEM((1, freqs), f32),
                pltpu.VMEM((n_rcv, 1, freqs), f32),
                pltpu.VMEM((1, freqs), f32),
                pltpu.VMEM((n_shot, 1, freqs), f32),
                dma((2,)),
                dma((parts,)),
                dma((parts, n_rcv - 1)),
                dma((parts, n_rcv - 1)),
                dma((parts, n_shot - 1)),
                dma((parts, n_shot - 1)),
                dma((n_rcv - 1,)),
                dma((n_rcv - 1,)),
                dma((n_shot - 1,)),
                dma((n_shot - 1,)),
                dma((n_rcv - 1,)),
                dma((n_rcv - 1,)),
                dma((n_shot - 1,)),
                dma((n_shot - 1,)),
            ],
            compiler_params=pltpu.CompilerParams(collective_id=0, has_side_effects=True),
        )(modeled, observed, coupling, mask, shot_order, line_of_slot, wavelet, damping[None, :])

    placed = (
        P(None, "shot", None, "rcv", None),
        P(None, "shot", "rcv", None, None),
        P("shot", None, "rcv"),
        P(),
        P(),
        P(),
        P(),
        P(),
    )
    return jax.shard_map(
        per_device,
        mesh=mesh,
        in_specs=placed,
        out_specs=(P(), P(None, "shot", None, "rcv", None)),
        check_vma=False,
    )
```

time: 83 us -> 37.6 us (0.45)
  blocking collectives: 37.2 us -> 0 us
  Pallas kernels: 0 us -> 33.6 us
  waiting for transfers between devices: 19.8 us -> 0 us
  starting transfers between devices: 10.3 us -> 0 us
  matrix products: 4.33 us -> 0 us
  local copies, waits for them, and re-layouts: 6.43 us -> 3.15 us
  other arithmetic: 3.19 us -> 0 us
    psum x1 -> x0, blocking collectives: 37.2 us -> none  [per_device(): numerator, den = lax.psum((numerator, den), ('shot', 'rcv'))]
    pallas_call x0 -> x1, Pallas kernels: none -> 33.6 us  [per_device(): pl.pallas_call(functools.partial(kernel, n_shot, n_rcv), out_shape=(jax.S...]
    all_to_all x2 -> x0, waiting for transfers between devices: 19.8 us -> none  [the longest x1 12.5 us: per_device(): lax.all_to_all(stored, 'rcv', split_axis=2, concat_axis=1, tiled=True)]
    all_to_all x2 -> x0, starting transfers between devices: 10.3 us -> none  [the longest x1 6.49 us: per_device(): lax.all_to_all(stored, 'rcv', split_axis=2, concat_axis=1, tiled=True)]
    dot_general x8 -> x0, matrix products: 4.33 us -> none  [the longest x2 1.73 us: weigh(): jnp.dot(trace[1], coupling[0], preferred_element_type=jnp.float32)]
    another operation x3 -> x0, other arithmetic: 2.11 us -> none  [the longest x2 2.1 us: per_device(): return (new_wavelet, jnp.stack([out_re, out_im]).astype(jnp.bfloat16))]
    unnamed x19 -> x2, local copies, waits for them, and re-layouts: 4.35 us -> 3.15 us
    gather x2 -> x0, local copies, waits for them, and re-layouts: 1.16 us -> none  [the longest x1 0.58 us: per_device(): by_line = jnp.transpose(jnp.take(arrived, inverse, axis=1), (0, 2, 1, 3, 4))]
  transfers between devices with their start and end apart: 2 -> 0, of which waited for: 2 -> 0; matrix products, arithmetic and copies ran while one was open for 3% -> 0% of each run, Pallas kernels for 0% -> 0%
where the time goes in v1:
time: 37.6 us; the launch traced here: 37.3 us
  Pallas kernels  33.6 us (89%)
  local copies, waits for them, and re-layouts  3.15 us (8%)
  between operations  0.64 us (2%)
    pallas_call x1, Pallas kernels, per_device(): pl.pallas_call(functools.partial(kernel, n_shot, n_rcv), out_shape=(jax.S...  33.6 us
    unnamed x2, local copies, waits for them, and re-layouts  3.15 us

profile of v1, /device:TPU:0, one launch (start us, length us, event | category | flops | bytes accessed | tf_op | source)
XLA Modules:
  0.0 37.3 jit_solution(18364907729444203784)
XLA Ops:
  0.6 33.6 %shard_map.95 = (f32[2,512]{1,0:T(2,128)}, bf16[2,8,4,8,512]{4,3,2,1,0:T(8,128)(2,1)}) custom-call(bf16[2,8,4,8,512]{4,3,2,1,0:T(8,128)(2,1)} %modeled_hbm.1, bf16[2,1,4,64,512]{4,3,2,1,0:T(8,128)(2,1)} %observed_hbm.1, bf16[2,512,512]{2,1,0:T(8,128)(2,1)} %coupling_hbm.1, s32[8,4,8]{2,1,0:T(4,128)} %mask_ref.1, s32[32]{0:T(128)} %order_ref.1, s32[4]{0:T(128)} %slot_ref.1, ...), custom_call_target="tpu_custom_call" | custom-call | tf_op jit(solution)/shard_map/pallas_call | solution.py:298
  34.2 1.3 %copy.12 = f32[2,512]{1,0:T(2,128)} copy(f32[2,512]{1,0:T(2,128)} %get-tuple-element.4) | data formatting | bytes 8192
  35.5 1.9 %copy.13 = bf16[2,8,4,8,512]{4,3,2,1,0:T(8,128)(2,1)} copy(bf16[2,8,4,8,512]{4,3,2,1,0:T(8,128)(2,1)} %get-tuple-element.5) | data formatting | bytes 1048576

commit v2 on v1

--- a/solution.py
+++ b/solution.py
@@ -8,7 +8,22 @@
 from jax.sharding import PartitionSpec as P
 
 MESH = pl.DeviceIdType.MESH
+HBM = pltpu.MemorySpace.HBM
 PIECES = 2
+
+
+def peers_of(me, n):
+    if n & (n - 1):
+        return [lax.rem(me + d, n) for d in range(1, n)]
+    out = []
+    for j in range(1, n):
+        peer, bit = me, 1
+        while bit < n:
+            if j & bit:
+                peer = peer + bit * (1 - 2 * lax.rem(me // bit, 2))
+            bit *= 2
+        out.append(peer)
+    return out
 
 
 def kernel(
@@ -17,19 +32,25 @@
     modeled_hbm,
     observed_hbm,
     coupling_hbm,
+    mask_hbm,
+    order_hbm,
+    slot_hbm,
+    wavelet_hbm,
+    damping_hbm,
+    new_ref,
+    wg,
+    wdl,
     mask_ref,
     order_ref,
     slot_ref,
     wavelet_ref,
     damping_ref,
-    new_ref,
-    out_ref,
     mod,
+    obs,
     coup,
     spread,
     grouped,
     arrived,
-    wg,
     wd,
     live,
     num_mine,
@@ -62,8 +83,8 @@
     parts = len(spread)
     width = spread[0].shape[2]
 
-    rcv_peers = [lax.rem(me_r + d, n_rcv) for d in range(1, n_rcv)]
-    shot_peers = [lax.rem(me_s + d, n_shot) for d in range(1, n_shot)]
+    rcv_peers = peers_of(me_r, n_rcv)
+    shot_peers = peers_of(me_s, n_shot)
 
     barrier = pltpu.get_barrier_semaphore()
     for r in rcv_peers:
@@ -71,6 +92,22 @@
     for s in shot_peers:
         pl.semaphore_signal(barrier, inc=1, device_id=(s, me_r), device_id_type=MESH)
 
+    small = [
+        pltpu.make_async_copy(src, dst, load_sem.at[2 + i])
+        for i, (src, dst) in enumerate(
+            (
+                (mask_hbm, mask_ref),
+                (order_hbm, order_ref),
+                (slot_hbm, slot_ref),
+                (wavelet_hbm, wavelet_ref),
+                (damping_hbm, damping_ref),
+            )
+        )
+    ]
+    for copy in small:
+        copy.start()
+    load_obs = pltpu.make_async_copy(observed_hbm, obs, load_sem.at[7])
+    load_obs.start()
     load_mod = pltpu.make_async_copy(modeled_hbm, mod, load_sem.at[0])
     load_coup = pltpu.make_async_copy(coupling_hbm, coup, load_sem.at[1])
     load_mod.start()
@@ -78,10 +115,11 @@
 
     def piece(t, r):
         c, h = divmod(t, parts // 2)
-        return observed_hbm.at[
+        return obs.at[
             c, 0, :, pl.ds(pl.multiple_of(r * rows, rows), rows), pl.ds(h * width, width)
         ]
 
+    load_obs.wait()
     own = []
     for t in range(parts):
         copy = pltpu.make_async_copy(
@@ -152,6 +190,9 @@
         for d in range(1, n_rcv):
             spread_copy(t, d).start()
 
+    for copy in small:
+        copy.wait()
+
     eye = (
         lax.broadcasted_iota(jnp.int32, (rows, rows), 0)
         == lax.broadcasted_iota(jnp.int32, (rows, rows), 1)
@@ -171,18 +212,22 @@
     tall = size * lines * rows
     x_re = mod[0].reshape(tall, freqs)
     x_im = mod[1].reshape(tall, freqs)
-    wg[0] = (dot(x_re, coup[0]) - dot(x_im, coup[1])).reshape(size * lines, rows, freqs)
-    wg[1] = (dot(x_re, coup[1]) + dot(x_im, coup[0])).reshape(size * lines, rows, freqs)
-
     wide = freqs // live.shape[2]
 
     def live_of(i):
         flag = live[i]
         return jnp.concatenate([flag] * wide, axis=1)
 
+    wg[0] = (dot(x_re, coup[0]) - dot(x_im, coup[1])).reshape(size * lines, rows, freqs)
+    wg[1] = (dot(x_re, coup[1]) + dot(x_im, coup[0])).reshape(size * lines, rows, freqs)
+
     den = jnp.zeros((rows, freqs), jnp.float32)
     for i in range(size * lines):
-        den = den + live_of(i) * (wg[0, i] * wg[0, i] + wg[1, i] * wg[1, i])
+        flag = live_of(i)
+        g_re, g_im = flag * wg[0, i], flag * wg[1, i]
+        wg[0, i] = g_re
+        wg[1, i] = g_im
+        den = den + (g_re * g_re + g_im * g_im)
     den_mine[...] = jnp.sum(den, axis=0, keepdims=True)
     den_rcv[me_r] = den_mine[...]
     rcv_sum(den_mine, den_rcv, den_send1, den_recv1, True)
@@ -246,8 +291,12 @@
             i = p * lines + l
             g_re, g_im, flag = wg[0, i], wg[1, i], live_of(i)
             at = slice(p * rows, (p + 1) * rows)
-            res_re = flag * (wd[0, slot_of[l], at, :] - (w_re * g_re - w_im * g_im))
-            res_im = flag * (wd[1, slot_of[l], at, :] - (w_re * g_im + w_im * g_re))
+            d_re = flag * wd[0, slot_of[l], at, :]
+            d_im = flag * wd[1, slot_of[l], at, :]
+            wdl[0, i] = d_re
+            wdl[1, i] = d_im
+            res_re = d_re - (w_re * g_re - w_im * g_im)
+            res_im = d_im - (w_re * g_im + w_im * g_re)
             num_re = num_re + (g_re * res_re + g_im * res_im)
             num_im = num_im + (g_re * res_im - g_im * res_re)
     num_mine[0:1, :] = jnp.sum(num_re, axis=0, keepdims=True)
@@ -264,22 +313,22 @@
     new = wavelet_ref[...] + total(num_shot, n_shot) / scale
     new_ref[...] = new
 
-    n_re, n_im = new[0:1, :], new[1:2, :]
-    for p in range(size):
-        for l in range(lines):
-            i = p * lines + l
-            g_re, g_im, flag = wg[0, i], wg[1, i], live_of(i)
-            at = slice(p * rows, (p + 1) * rows)
-            out_re = flag * (wd[0, slot_of[l], at, :] - (n_re * g_re - n_im * g_im))
-            out_im = flag * (wd[1, slot_of[l], at, :] - (n_re * g_im + n_im * g_re))
-            out_ref[0, p, l] = out_re.astype(jnp.bfloat16)
-            out_ref[1, p, l] = out_im.astype(jnp.bfloat16)
-
     for t in range(parts):
         for d in range(1, n_rcv):
             spread_copy(t, d).wait_send()
         for d in range(1, n_shot):
             group_copy(t, d).wait_send()
+
+
+def finish(new_ref, wg, wdl, wave_out, out_ref):
+    lines = out_ref.shape[2]
+    wave_out[...] = new_ref[...]
+    n_re, n_im = new_ref[0:1, :], new_ref[1:2, :]
+    for i in range(wg.shape[1]):
+        g_re, g_im = wg[0, i], wg[1, i]
+        p, l = divmod(i, lines)
+        out_ref[0, p, l] = (wdl[0, i] - (n_re * g_re - n_im * g_im)).astype(jnp.bfloat16)
+        out_ref[1, p, l] = (wdl[1, i] - (n_re * g_im + n_im * g_re)).astype(jnp.bfloat16)
 
 
 def solution(mesh):
@@ -292,24 +341,29 @@
         width = freqs // PIECES
         f32, bf16 = jnp.float32, jnp.bfloat16
         dma = pltpu.SemaphoreType.DMA
-        any_ = pl.BlockSpec(memory_space=pl.ANY)
+        hbm = pl.BlockSpec(memory_space=HBM)
         vmem = pl.BlockSpec(memory_space=pltpu.VMEM)
-        smem = pl.BlockSpec(memory_space=pltpu.SMEM)
-        return pl.pallas_call(
+        new, wg, wdl = pl.pallas_call(
             functools.partial(kernel, n_shot, n_rcv),
             out_shape=(
-                jax.ShapeDtypeStruct(wavelet.shape, f32),
-                jax.ShapeDtypeStruct(modeled.shape, bf16),
+                pltpu.VMEM(wavelet.shape, f32),
+                pltpu.VMEM((2, size * lines, rows, freqs), f32),
+                pltpu.VMEM((2, size * lines, rows, freqs), f32),
             ),
-            in_specs=[any_, any_, any_, vmem, smem, smem, vmem, vmem],
-            out_specs=(vmem, vmem),
+            in_specs=[hbm] * 8,
+            out_specs=(vmem, vmem, vmem),
             scratch_shapes=[
+                pltpu.VMEM(mask.shape, jnp.int32),
+                pltpu.SMEM(shot_order.shape, jnp.int32),
+                pltpu.SMEM(line_of_slot.shape, jnp.int32),
+                pltpu.VMEM(wavelet.shape, f32),
+                pltpu.VMEM((1, freqs), f32),
                 pltpu.VMEM(modeled.shape, bf16),
+                pltpu.VMEM(observed.shape, bf16),
                 pltpu.VMEM(coupling.shape, bf16),
                 [pltpu.VMEM((shots, rows, width), bf16)] * parts,
                 pltpu.VMEM((parts, n_shot - 1, size * rows, width), bf16),
                 pltpu.VMEM((parts, n_shot, size * rows, width), bf16),
-                pltpu.VMEM((2, size * lines, rows, freqs), f32),
                 pltpu.VMEM((2, n_shot, size * rows, freqs), f32),
                 pltpu.VMEM((size * lines, rows, 128), f32),
                 pltpu.VMEM((2, freqs), f32),
@@ -320,7 +374,7 @@
                 pltpu.VMEM((n_rcv, 1, freqs), f32),
                 pltpu.VMEM((1, freqs), f32),
                 pltpu.VMEM((n_shot, 1, freqs), f32),
-                dma((2,)),
+                dma((8,)),
                 dma((parts,)),
                 dma((parts, n_rcv - 1)),
                 dma((parts, n_rcv - 1)),
@@ -335,8 +389,22 @@
                 dma((n_shot - 1,)),
                 dma((n_shot - 1,)),
             ],
-            compiler_params=pltpu.CompilerParams(collective_id=0, has_side_effects=True),
+            compiler_params=pltpu.CompilerParams(
+                collective_id=0,
+                has_side_effects=True,
+                vmem_limit_bytes=modeled.size * 48 + coupling.size * 8,
+            ),
         )(modeled, observed, coupling, mask, shot_order, line_of_slot, wavelet, damping[None, :])
+        return pl.pallas_call(
+            finish,
+            out_shape=(
+                jax.ShapeDtypeStruct(wavelet.shape, f32),
+                jax.ShapeDtypeStruct(modeled.shape, bf16),
+            ),
+            in_specs=[vmem] * 3,
+            out_specs=(vmem, vmem),
+            compiler_params=pltpu.CompilerParams(vmem_limit_bytes=modeled.size * 16 + (1 << 21)),
+        )(*(pltpu.with_memory_space_constraint(x, pltpu.VMEM) for x in (new, wg, wdl)))
 
     placed = (
         P(None, "shot", None, "rcv", None),

time: 37.6 us -> 39.7 us (1.056)
  local copies, waits for them, and re-layouts: 3.15 us -> 6.05 us
  Pallas kernels: 33.6 us -> 32.6 us
    unnamed x2 -> x16, local copies, waits for them, and re-layouts: 3.15 us -> 6.05 us
    pallas_call x1 -> x2, Pallas kernels: 33.6 us -> 32.6 us  [the longest x1 31.7 us: per_device(): pl.pallas_call(functools.partial(kernel, n_shot, n_rcv), out_shape=(pltpu...]
where the time goes in v2:
time: 39.7 us; the launch traced here: 39.3 us
  Pallas kernels  32.6 us (82%)
  local copies, waits for them, and re-layouts  6.05 us (15%)
  between operations  0.66 us (2%)
    pallas_call x1, Pallas kernels, per_device(): pl.pallas_call(functools.partial(kernel, n_shot, n_rcv), out_shape=(pltpu...  31.7 us
    unnamed x16, local copies, waits for them, and re-layouts  6.05 us
    pallas_call x1, Pallas kernels, per_device(): pl.pallas_call(finish, out_shape=(jax.ShapeDtypeStruct(wavelet.shape, f32...  0.96 us

profile of v2, /device:TPU:0, one launch (start us, length us, event | category | flops | bytes accessed | tf_op | source)
XLA Modules:
  0.0 39.3 jit_solution(15428780977175053050)
XLA Ops:
  0.6 0.0 copy-start.7
  0.6 0.0 copy-start.6
  0.7 0.6 %copy-done.7 = s32[4]{0:T(128)S(1)} copy-done((s32[4]{0:T(128)S(1)}, s32[4]{0:T(128)}, u32[]{:S(2)}) %copy-start.7) | copy-done | bytes 40
  1.3 0.0 copy-done.6
  1.3 0.0 copy-start
  1.3 1.2 %copy-done = bf16[2,512,512]{2,1,0:T(8,128)(2,1)S(1)} copy-done((bf16[2,512,512]{2,1,0:T(8,128)(2,1)S(1)}, bf16[2,512,512]{2,1,0:T(8,128)(2,1)}, u32[]{:S(2)}) %copy-start) | copy-done | bytes 1048600
  2.5 0.0 copy-start.1
  2.5 1.0 %copy-done.1 = bf16[2,8,4,8,512]{4,3,2,1,0:T(8,128)(2,1)S(1)} copy-done((bf16[2,8,4,8,512]{4,3,2,1,0:T(8,128)(2,1)S(1)}, bf16[2,8,4,8,512]{4,3,2,1,0:T(8,128)(2,1)}, u32[]{:S(2)}) %copy-start.1) | copy-done | bytes 524312
  3.6 0.0 copy-start.2
  3.6 1.0 %copy-done.2 = bf16[2,1,4,64,512]{4,3,2,1,0:T(8,128)(2,1)S(1)} copy-done((bf16[2,1,4,64,512]{4,3,2,1,0:T(8,128)(2,1)S(1)}, bf16[2,1,4,64,512]{4,3,2,1,0:T(8,128)(2,1)}, u32[]{:S(2)}) %copy-start.2) | copy-done | bytes 524312
  4.6 0.0 copy-start.3
  4.6 0.7 %copy-done.3 = s32[8,4,8]{2,1,0:T(4,128)S(1)} copy-done((s32[8,4,8]{2,1,0:T(4,128)S(1)}, s32[8,4,8]{2,1,0:T(4,128)}, u32[]{:S(2)}) %copy-start.3) | copy-done | bytes 1048
  5.3 0.0 copy-start.4
  5.3 0.7 %copy-done.4 = f32[2,512]{1,0:T(2,128)S(1)} copy-done((f32[2,512]{1,0:T(2,128)S(1)}, f32[2,512]{1,0:T(2,128)}, u32[]{:S(2)}) %copy-start.4) | copy-done | bytes 4120
  6.0 0.0 copy-start.5
  6.0 0.7 %copy-done.5 = f32[512]{0:T(512)S(1)} copy-done((f32[512]{0:T(512)S(1)}, f32[512]{0:T(512)}, u32[]{:S(2)}) %copy-start.5) | copy-done | bytes 2072
  6.7 31.7 %shard_map.95 = (f32[2,512]{1,0:T(2,128)S(1)}, f32[2,32,8,512]{3,2,1,0:T(8,128)S(1)}, f32[2,32,8,512]{3,2,1,0:T(8,128)S(1)}) custom-call(bf16[2,8,4,8,512]{4,3,2,1,0:T(8,128)(2,1)S(1)} %copy-done.1, bf16[2,1,4,64,512]{4,3,2,1,0:T(8,128)(2,1)S(1)} %copy-done.2, bf16[2,512,512]{2,1,0:T(8,128)(2,1)S(1)} %copy-done, s32[8,4,8]{2,1,0:T(4,128)S(1)} %copy-done.3, ...), custom_call_target="tpu_custom_call" | custom-call | tf_op jit(solution)/shard_map/pallas_call | solution.py:346
  38.4 1.0 %shard_map.96 = (f32[2,512]{1,0:T(2,128)}, bf16[2,8,4,8,512]{4,3,2,1,0:T(8,128)(2,1)}) custom-call(f32[2,512]{1,0:T(2,128)S(1)} %get-tuple-element.5.new_ref, f32[2,32,8,512]{3,2,1,0:T(8,128)S(1)} %get-tuple-element.6.wg, f32[2,32,8,512]{3,2,1,0:T(8,128)S(1)} %get-tuple-element.7.wdl), custom_call_target="tpu_custom_call" | custom-call | tf_op jit(solution)/shard_map/pallas_call | solution.py:398
Async XLA Ops:
  0.6 0.7 %copy-start.7 = (s32[4]{0:T(128)S(1)}, s32[4]{0:T(128)}, u32[]{:S(2)}) copy-start(s32[4]{0:T(128)} %slot_hbm.1) | copy-start | bytes 52
  0.6 0.7 %copy-start.6 = (s32[32]{0:T(128)S(1)}, s32[32]{0:T(128)}, u32[]{:S(2)}) copy-start(s32[32]{0:T(128)} %order_hbm.1) | copy-start | bytes 388
  1.3 1.2 %copy-start = (bf16[2,512,512]{2,1,0:T(8,128)(2,1)S(1)}, bf16[2,512,512]{2,1,0:T(8,128)(2,1)}, u32[]{:S(2)}) copy-start(bf16[2,512,512]{2,1,0:T(8,128)(2,1)} %coupling_hbm.1) | copy-start | bytes 3145732
  2.5 1.0 %copy-start.1 = (bf16[2,8,4,8,512]{4,3,2,1,0:T(8,128)(2,1)S(1)}, bf16[2,8,4,8,512]{4,3,2,1,0:T(8,128)(2,1)}, u32[]{:S(2)}) copy-start(bf16[2,8,4,8,512]{4,3,2,1,0:T(8,128)(2,1)} %modeled_hbm.1) | copy-start | bytes 1572868
  3.6 1.0 %copy-start.2 = (bf16[2,1,4,64,512]{4,3,2,1,0:T(8,128)(2,1)S(1)}, bf16[2,1,4,64,512]{4,3,2,1,0:T(8,128)(2,1)}, u32[]{:S(2)}) copy-start(bf16[2,1,4,64,512]{4,3,2,1,0:T(8,128)(2,1)} %observed_hbm.1) | copy-start | bytes 1572868
  4.6 0.7 %copy-start.3 = (s32[8,4,8]{2,1,0:T(4,128)S(1)}, s32[8,4,8]{2,1,0:T(4,128)}, u32[]{:S(2)}) copy-start(s32[8,4,8]{2,1,0:T(4,128)} %mask_hbm.1) | copy-start | bytes 3076
  5.3 0.7 %copy-start.4 = (f32[2,512]{1,0:T(2,128)S(1)}, f32[2,512]{1,0:T(2,128)}, u32[]{:S(2)}) copy-start(f32[2,512]{1,0:T(2,128)} %wavelet_hbm.1) | copy-start | bytes 12292
  6.0 0.7 %copy-start.5 = (f32[512]{0:T(512)S(1)}, f32[512]{0:T(512)}, u32[]{:S(2)}) copy-start(f32[512]{0:T(512)} %param.15) | copy-start | bytes 6148

commit v3 on v2

--- a/solution.py
+++ b/solution.py
@@ -392,7 +392,7 @@
             compiler_params=pltpu.CompilerParams(
                 collective_id=0,
                 has_side_effects=True,
-                vmem_limit_bytes=modeled.size * 48 + coupling.size * 8,
+                vmem_limit_bytes=min(60 * 1024 * 1024, (63 << 20) - modeled.size * 8),
             ),
         )(modeled, observed, coupling, mask, shot_order, line_of_slot, wavelet, damping[None, :])
         return pl.pallas_call(

time: 39.7 us -> 33 us (0.83)
  local copies, waits for them, and re-layouts: 6.05 us -> 0 us
  Pallas kernels: 32.6 us -> 32.2 us
    unnamed x16 -> x0, local copies, waits for them, and re-layouts: 6.05 us -> none
    pallas_call x1, Pallas kernels: 31.7 us -> 31.2 us  [per_device(): pl.pallas_call(functools.partial(kernel, n_shot, n_rcv), out_shape=(pltpu...]
where the time goes in v3:
time: 33 us; the launch traced here: 32.8 us
  Pallas kernels  32.2 us (98%)
  between operations  0.64 us (2%)
    pallas_call x1, Pallas kernels, per_device(): pl.pallas_call(functools.partial(kernel, n_shot, n_rcv), out_shape=(pltpu...  31.2 us
    pallas_call x1, Pallas kernels, per_device(): pl.pallas_call(finish, out_shape=(jax.ShapeDtypeStruct(wavelet.shape, f32...  0.96 us

profile of v3, /device:TPU:0, one launch (start us, length us, event | category | flops | bytes accessed | tf_op | source)
XLA Modules:
  0.0 32.8 jit_solution(8953905754262143213)
XLA Ops:
  0.6 31.2 %shard_map.95 = (f32[2,512]{1,0:T(2,128)S(1)}, f32[2,32,8,512]{3,2,1,0:T(8,128)S(1)}, f32[2,32,8,512]{3,2,1,0:T(8,128)S(1)}) custom-call(bf16[2,8,4,8,512]{4,3,2,1,0:T(8,128)(2,1)} %modeled_hbm.1, bf16[2,1,4,64,512]{4,3,2,1,0:T(8,128)(2,1)} %observed_hbm.1, bf16[2,512,512]{2,1,0:T(8,128)(2,1)} %coupling_hbm.1, s32[8,4,8]{2,1,0:T(4,128)} %mask_hbm.1, ...), custom_call_target="tpu_custom_call" | custom-call | tf_op jit(solution)/shard_map/pallas_call | solution.py:346
  31.9 1.0 %shard_map.96 = (f32[2,512]{1,0:T(2,128)}, bf16[2,8,4,8,512]{4,3,2,1,0:T(8,128)(2,1)}) custom-call(f32[2,512]{1,0:T(2,128)S(1)} %get-tuple-element.5.new_ref, f32[2,32,8,512]{3,2,1,0:T(8,128)S(1)} %get-tuple-element.6.wg, f32[2,32,8,512]{3,2,1,0:T(8,128)S(1)} %get-tuple-element.7.wdl), custom_call_target="tpu_custom_call" | custom-call | tf_op jit(solution)/shard_map/pallas_call | solution.py:398

commit v4 on v3

--- a/solution.py
+++ b/solution.py
@@ -256,6 +256,9 @@
         for d in range(1, n_rcv):
             spread_copy(t, d).wait_recv()
         for d in list(range(1, n_shot)) + [0]:
+            if d == 0:
+                for e in range(1, n_shot):
+                    group_copy(t, e).start()
             group = shot_peers[d - 1] if d else me_s
             for p in range(0, size, 2):
                 first = order_ref[group * size + p]
@@ -265,8 +268,6 @@
                     grouped[t, d - 1, p * rows : (p + 2) * rows, :] = pair
                 else:
                     arrived[t, me_s, p * rows : (p + 2) * rows, :] = pair
-        for d in range(1, n_shot):
-            group_copy(t, d).start()
         if t == parts - 1:
             rcv_sum(den_mine, den_rcv, den_send1, den_recv1, False)
             den_group[...] = total(den_rcv, n_rcv)

time: 33 us -> 33 us (level)
  no operation moved by 1% of the time
where the time goes in v4:
time: 33 us; the launch traced here: 32.8 us
  Pallas kernels  32.2 us (98%)
  between operations  0.64 us (2%)
    pallas_call x1, Pallas kernels, per_device(): pl.pallas_call(functools.partial(kernel, n_shot, n_rcv), out_shape=(pltpu...  31.2 us
    pallas_call x1, Pallas kernels, per_device(): pl.pallas_call(finish, out_shape=(jax.ShapeDtypeStruct(wavelet.shape, f32...  0.96 us

profile of v4, /device:TPU:0, one launch (start us, length us, event | category | flops | bytes accessed | tf_op | source)
XLA Modules:
  0.0 32.8 jit_solution(17424038496967846492)
XLA Ops:
  0.6 31.2 %shard_map.95 = (f32[2,512]{1,0:T(2,128)S(1)}, f32[2,32,8,512]{3,2,1,0:T(8,128)S(1)}, f32[2,32,8,512]{3,2,1,0:T(8,128)S(1)}) custom-call(bf16[2,8,4,8,512]{4,3,2,1,0:T(8,128)(2,1)} %modeled_hbm.1, bf16[2,1,4,64,512]{4,3,2,1,0:T(8,128)(2,1)} %observed_hbm.1, bf16[2,512,512]{2,1,0:T(8,128)(2,1)} %coupling_hbm.1, s32[8,4,8]{2,1,0:T(4,128)} %mask_hbm.1, ...), custom_call_target="tpu_custom_call" | custom-call | tf_op jit(solution)/shard_map/pallas_call | solution.py:347
  31.8 1.0 %shard_map.96 = (f32[2,512]{1,0:T(2,128)}, bf16[2,8,4,8,512]{4,3,2,1,0:T(8,128)(2,1)}) custom-call(f32[2,512]{1,0:T(2,128)S(1)} %get-tuple-element.5.new_ref, f32[2,32,8,512]{3,2,1,0:T(8,128)S(1)} %get-tuple-element.6.wg, f32[2,32,8,512]{3,2,1,0:T(8,128)S(1)} %get-tuple-element.7.wdl), custom_call_target="tpu_custom_call" | custom-call | tf_op jit(solution)/shard_map/pallas_call | solution.py:399
